TPU v7x, 32 devices: a whole 2x2x4 slice. The times are simulated.
32 devices in a mesh: dom: 32 (over z, y, x, core).
Axes of the slice: x: 2, y: 2, z: 4, core: 2. Of those that a mesh axis runs over, the one named last changes fastest.
Arguments:
- entities: float32 [32768, 200], P('dom'), may hold values from -3 to 3
- entity_state: float32 [32768], P('dom'), may hold values from 1e-05 to 0.1
- relations: float32 [1345, 200], replicated, may hold values from -3 to 3
- relation_state: float32 [1345], replicated, may hold values from 1 to 100
- edges: int32 [2, 3, 16384], P(None, None, 'dom'), may hold values from 0 to 1344, as said below
- negatives: int32 [2, 128, 1000], P(None, 'dom'), may hold values from 0 to 1023
- counts: int32 [2, 32], P(None, 'dom'), may hold values from 1 to 512, as said below
Outputs:
- entities_after: float32 [32768, 200], P('dom')
- entity_state_after: float32 [32768], P('dom')
- relations_after: float32 [1345, 200], replicated
- relation_state_after: float32 [1345], replicated
Inputs may be any that keep to these rules, and one draw needn't show every extreme that they name: `edges`: rows 0 and 2 are local entity ids below 1024; row 1 holds relation ids below 1345. `negatives`: local ids in the partner's partition. `counts`: in every round some bucket is full.
All inputs are finite; a program needn't handle non-finite values.
Results may differ from a plain program's by a relative error of at most 0.0003.
Values sent between devices are 32-bit elements; how exact they have to be, the bound alone decides.
A program may use at most 64 MiB of HBM per device.

v0:
```python
import jax
import jax.numpy as jnp
from jax import lax
from jax.sharding import PartitionSpec as P

RATE = 0.2
HIGH = lax.Precision.HIGHEST


def swapped(block, axis, apart):
    count = lax.axis_size(axis)
    route = []
    for low in range(count):
        high = low | 1 << apart
        if high != low and high < count:
            route += [(low, high), (high, low)]
    return lax.ppermute(block, axis, route)


def block_terms(carry, table, relations, source, relation, target, negative_ids, live):
    grad_table, grad_relation = carry
    half = table.shape[1] // 2
    src_rows = table[source]
    tgt_rows = table[target]
    neg_rows = table[negative_ids]
    rel_rows = relations[relation]
    src_real, src_imag = (src_rows[:, :half], src_rows[:, half:])
    rel_real, rel_imag = (rel_rows[:, :half], rel_rows[:, half:])
    product = jnp.concatenate(
        [src_real * rel_real - src_imag * rel_imag, src_real * rel_imag + src_imag * rel_real],
        axis=1,
    )
    positive = jnp.sum(product * tgt_rows, axis=1)
    negative = lax.dot_general(
        product,
        neg_rows,
        (((1,), (1,)), ((), ())),
        precision=HIGH,
        preferred_element_type=jnp.float32,
    )
    pos_weight = -jax.nn.sigmoid(-positive) * live
    neg_weight = jax.nn.sigmoid(negative) * (live[:, None] / negative.shape[1])
    upstream = pos_weight[:, None] * tgt_rows + jnp.dot(
        neg_weight, neg_rows, precision=HIGH, preferred_element_type=jnp.float32
    )
    target_grad = pos_weight[:, None] * product
    negative_grad = lax.dot_general(
        neg_weight,
        product,
        (((0,), (0,)), ((), ())),
        precision=HIGH,
        preferred_element_type=jnp.float32,
    )
    up_real, up_imag = (upstream[:, :half], upstream[:, half:])
    source_grad = jnp.concatenate(
        [up_real * rel_real + up_imag * rel_imag, up_imag * rel_real - up_real * rel_imag], axis=1
    )
    relation_grad = jnp.concatenate(
        [up_real * src_real + up_imag * src_imag, up_imag * src_real - up_real * src_imag], axis=1
    )
    grad_table = (
        grad_table.at[source]
        .add(source_grad)
        .at[target]
        .add(target_grad)
        .at[negative_ids]
        .add(negative_grad)
    )
    grad_relation = grad_relation.at[relation].add(relation_grad)
    return (grad_table, grad_relation)


def bucket_pass(
    carry,
    table,
    relations,
    edge_pair,
    negative_pair,
    count_pair,
    source_shift,
    target_shift,
    block,
    first,
    last,
):
    block_pair = (count_pair + block - 1) // block

    def visit(index, inner):
        which = (index >= block_pair[0]).astype(jnp.int32)
        number = index - which * block_pair[0]
        edge_list = lax.dynamic_index_in_dim(edge_pair, which, 0, keepdims=False)
        start = number * block
        window = lax.dynamic_slice_in_dim(edge_list, start, block, 1)
        negative_list = lax.dynamic_index_in_dim(negative_pair, which, 0, keepdims=False)
        negative_ids = (
            lax.dynamic_index_in_dim(negative_list, number, 0, keepdims=False) + target_shift[which]
        )
        live = (start + jnp.arange(block, dtype=jnp.int32) < count_pair[which]).astype(jnp.float32)
        return block_terms(
            inner,
            table,
            relations,
            window[0] + source_shift[which],
            window[1],
            window[2] + target_shift[which],
            negative_ids,
            live,
        )

    return lax.fori_loop(first, last, visit, carry)


def adagrad(param, state, grad):
    new_state = state + jnp.mean(grad * grad, axis=1)
    return (param - RATE * grad / jnp.sqrt(new_state)[:, None], new_state)


def body(entities, entity_state, relations, relation_state, edges, negatives, counts):
    rows = entities.shape[0]
    blocks_dev = negatives.shape[1]
    block = edges.shape[2] // blocks_dev
    levels = lax.axis_size("dom").bit_length() - 1
    for round_index, bit in enumerate((levels - 1, 0)):
        partner = swapped(entities, "dom", bit)
        table = jnp.concatenate([entities, partner], axis=0)
        own_edges = edges[round_index]
        own_negatives = negatives[round_index]
        own_count = counts[round_index]
        other_edges, other_negatives, other_count = swapped(
            (own_edges, own_negatives, own_count), "dom", bit
        )
        upper = lax.axis_index("dom") // 2**bit % 2
        flipped = upper == 1
        edge_pair = jnp.where(
            flipped, jnp.stack([other_edges, own_edges]), jnp.stack([own_edges, other_edges])
        )
        negative_pair = jnp.where(
            flipped,
            jnp.stack([other_negatives, own_negatives]),
            jnp.stack([own_negatives, other_negatives]),
        )
        count_pair = jnp.where(
            flipped,
            jnp.concatenate([other_count, own_count]),
            jnp.concatenate([own_count, other_count]),
        )
        source_shift = jnp.stack([upper * rows, (1 - upper) * rows])
        target_shift = jnp.stack([(1 - upper) * rows, upper * rows])
        block_pair = (count_pair + block - 1) // block
        total = block_pair[0] + block_pair[1]
        middle = (total + 1) // 2
        first = upper * middle
        last = middle + upper * (total - middle)
        empty = (
            jnp.zeros((2 * rows, entities.shape[1]), jnp.float32),
            jnp.zeros(relations.shape, jnp.float32),
        )
        grads, relation_grads = bucket_pass(
            empty,
            table,
            relations,
            edge_pair,
            negative_pair,
            count_pair,
            source_shift,
            target_shift,
            block,
            first,
            last,
        )
        returned = swapped(grads[rows:], "dom", bit)
        relation_total = lax.psum(relation_grads, "dom")
        entities, entity_state = adagrad(entities, entity_state, grads[:rows] + returned)
        relations, relation_state = adagrad(relations, relation_state, relation_total)
    return (entities, entity_state, relations, relation_state)


def solution(mesh):
    return jax.shard_map(
        body,
        mesh=mesh,
        in_specs=(
            P("dom", None),
            P("dom"),
            P(),
            P(),
            P(None, None, "dom"),
            P(None, "dom", None),
            P(None, "dom"),
        ),
        out_specs=(P("dom", None), P("dom"), P(), P()),
        check_vma=False,
    )
```

profile of v0, /device:TPU:0, one launch (start us, length us, event | category | flops | bytes accessed | tf_op | source)
XLA Modules:
  0.0 608.5 jit_solution(12843747475687905343)
XLA Ops:
  7.2 1.3 fusion.30
  8.5 4.1 collective-permute-start
  12.6 1.4 fusion.28
  14.0 2.9 collective-permute-start.1
  16.9 1.3 slice_bitcast_fusion
  18.3 2.8 copy.91
  24.3 27.5 %collective-permute-done.1 = s32[3,512]{1,0:T(4,128)S(1)} collective-permute-done((s32[3,512]{1,0:T(4,128)S(1)}, s32[3,512]{1,0:T(4,128)S(1)}, u32[]{:S(2)}, u32[]{:S(2)}) %collective-permute-start.1) | collective-permute-done | bytes 6176 | tf_op jit(solution)/shard_map/ppermute | solution.py:17
  52.2 1.8 copy.90
  55.3 80.7 %while.30 = (s32[]{:T(128)}, f32[2048,200]{1,0:T(8,128)S(1)}, f32[1345,200]{1,0:T(8,128)}, s32[]{:T(128)}, s32[2]{0:T(128)S(1)}, /*index=5*/s32[2,3,512]{2,1,0:T...) while((s32[]{:T(128)}, f32[2048,200]{1,0:T(8,128)S(1)}, ...), condition=%wide.region_6.7_spmd, body=%wide.region_0.6_spmd.sunk | while | flops 922911104 | bytes 17251100 | solution.py:110
  59.4 2.1 gather_fusion.3
  61.8 2.4 gather_fusion.2
  64.3 2.3 gather_fusion
  68.3 5.2 gather_fusion.1
  73.5 1.7 fusion.65
  75.2 1.8 convolution_add_fusion.4
  78.6 2.0 fusion.66
  80.7 4.0 scatter_fusion.3
  84.6 2.0 scatter_fusion
  86.7 2.0 scatter_fusion.1
  88.8 6.8 %scatter_fusion.2 = f32[2048,200]{1,0:T(8,128)S(1)} fusion(f32[2048,200]{1,0:T(8,128)S(1)} %scatter_fusion.1, s32[1000]{0:T(1024)S(1)} %bitcast.123, f32[1000,200]{1,0:T(8,128)S(1)} %fusion.66), kind=kCustom, calls=%fused_computation.10.clone.1 | custom fusion | flops 200000 | bytes 2404000 | tf_op jit(solution)/shard_map/while/body/scatter-add | solution.py:67
  99.7 2.1 gather_fusion.3
  102.2 2.4 gather_fusion.2
  104.6 2.3 gather_fusion
  108.6 5.2 gather_fusion.1
  113.8 1.7 fusion.65
  115.5 1.8 convolution_add_fusion.4
  118.9 2.0 fusion.66
  121.0 4.0 scatter_fusion.3
  125.0 2.0 scatter_fusion
  127.0 2.0 scatter_fusion.1
  129.1 6.8 %scatter_fusion.2 = f32[2048,200]{1,0:T(8,128)S(1)} fusion(f32[2048,200]{1,0:T(8,128)S(1)} %scatter_fusion.1, s32[1000]{0:T(1024)S(1)} %bitcast.123, f32[1000,200]{1,0:T(8,128)S(1)} %fusion.66), kind=kCustom, calls=%fused_computation.10.clone.1 | custom fusion | flops 200000 | bytes 2404000 | tf_op jit(solution)/shard_map/while/body/scatter-add | solution.py:67
  136.0 1.7 copy.92
  137.8 2.2 slice.233
  141.4 1.9 and_select_fusion
  143.3 1.3 fusion.29
  147.2 1.4 copy.95
  148.7 20.0 %collective-permute-done.4 = f32[1024,200]{0,1:T(8,128)} collective-permute-done((f32[1024,200]{0,1:T(8,128)}, f32[1024,200]{0,1:T(8,128)}, u32[]{:S(2)}, u32[]{:S(2)}) %collective-permute-start.4) | collective-permute-done | bytes 819232 | tf_op jit(solution)/shard_map/ppermute | solution.py:17
  170.0 2.3 divide_subtract_fusion.3
  172.3 145.7 %all-reduce.3.cloned.1.call-done = f32[1345,200]{0,1:T(8,128)} async-done(((f32[1345,200]{0,1:T(8,128)}), f32[1345,200]{0,1:T(8,128)}) %all-reduce.3.cloned.1.call-update) | async-done | bytes 1076016 | tf_op jit(solution)/shard_map/psum | solution.py:172
  318.1 1.3 multiply_reduce_fusion.3
  319.5 1.4 divide_subtract_fusion.1
  320.9 1.5 copy.97
  322.4 1.5 pad_maximum_fusion.11
  324.0 1.8 copy.96
  327.1 44.8 %while.31 = (s32[]{:T(128)}, f32[2048,200]{1,0:T(8,128)S(1)}, f32[1345,200]{1,0:T(8,128)}, s32[]{:T(128)}, s32[2]{0:T(128)}, /*index=5*/s32[2,3,512]{2,1,0:T(4,1...) while((s32[]{:T(128)}, f32[2048,200]{1,0:T(8,128)S(1)}, ...), condition=%wide.region_16.17_spmd, body=%wide.region_10.16_spmd.sunk | while | flops 922911104 | bytes 16896204 | solution.py:110
  333.0 1.3 fusion.71
  334.4 1.4 compare_select_fusion.24
  335.8 2.1 gather_fusion.7
  338.2 2.4 gather_fusion.6
  340.7 2.3 gather_fusion.4
  344.6 5.2 gather_fusion.5
  349.9 1.7 fusion.74
  351.6 1.8 convolution_add_fusion.5
  355.0 2.0 fusion.75
  357.0 4.0 scatter_fusion.7
  361.0 2.0 scatter_fusion.4
  363.0 2.0 scatter_fusion.5
  365.1 6.8 %scatter_fusion.6 = f32[2048,200]{1,0:T(8,128)S(1)} fusion(f32[2048,200]{1,0:T(8,128)S(1)} %scatter_fusion.5, s32[1000]{0:T(1024)S(1)} %bitcast.125, f32[1000,200]{1,0:T(8,128)S(1)} %fusion.75), kind=kCustom, calls=%fused_computation.14.clone.1 | custom fusion | flops 200000 | bytes 2404000 | tf_op jit(solution)/shard_map/while/body/scatter-add | solution.py:67
  371.9 2.8 copy.100
  374.7 1.7 copy.98
  376.5 1.3 slice.235
  377.9 216.9 %all-reduce.5.cloned.1.call-done = f32[1345,200]{0,1:T(8,128)} async-done(((f32[1345,200]{0,1:T(8,128)}), f32[1345,200]{0,1:T(8,128)}) %all-reduce.5.cloned.1.call-update) | async-done | bytes 1076016 | tf_op jit(solution)/shard_map/psum | solution.py:172
  594.7 1.4 multiply_reduce_fusion.2
  599.4 2.3 divide_subtract_fusion.2
  (245 shorter events, 35.2 us)
Async XLA Ops:
  7.2 44.9 %copy-start.23 = (f32[1024,200]{0,1:T(8,128)S(1)}, f32[1024,200]{0,1:T(8,128)}, u32[]{:S(2)}) copy-start(f32[1024,200]{0,1:T(8,128)} %param.11) | copy-start | bytes 2457604
  7.2 310.9 %all-reduce.3.cloned.1.call-start = ((), (), s32[]{:S(2)}) async-start(), calls=%async_computation | async-start | bytes 2252800 | tf_op jit(solution)/shard_map/psum | solution.py:172
  8.5 12.6 %collective-permute-start = (s32[1]{0:T(128)}, s32[1]{0:T(128)}, u32[]{:S(2)}, u32[]{:S(2)}) collective-permute-start(s32[1]{0:T(128)} %bitcast.24), channel_id=1, source_target_pairs={{0,16},{16,0},{1,17},{17,1},{2,18},{18,2},{3,19},{19,3},{4,20},{20... | collective-permute-start | bytes 20 | tf_op jit(solution)/shard_map/ppermute | solution.py:17
  12.6 39.4 %collective-permute-start.2 = (f32[1024,200]{0,1:T(8,128)}, f32[1024,200]{0,1:T(8,128)S(1)}, u32[]{:S(2)}, u32[]{:S(2)}) collective-permute-start(f32[1024,200]{0,1:T(8,128)} %param.11), channel_id=1, source_target_pairs={{0,16},{16,0},{1,17},{17,1},{2,18},{18,2},{3,19},{19,3},{4,20},{20... | collective-permute-start | bytes 2457608 | tf_op jit(solution)/shard_map/ppermute | solution.py:17
  14.0 37.8 %collective-permute-start.1 = (s32[3,512]{1,0:T(4,128)S(1)}, s32[3,512]{1,0:T(4,128)S(1)}, u32[]{:S(2)}, u32[]{:S(2)}) collective-permute-start(s32[3,512]{1,0:T(4,128)S(1)} %bitcast.126), channel_id=1, source_target_pairs={{0,16},{16,0},{1,17},{17,1},{2,18},{18,2},{3,19},{19,3},{4,20},{20... | collective-permute-start | bytes 18440 | tf_op jit(solution)/shard_map/ppermute | solution.py:17
  18.3 33.8 %collective-permute-start.3 = (s32[4,1000]{1,0:T(4,128)S(1)}, s32[4,1000]{1,0:T(4,128)S(1)}, u32[]{:S(2)}, u32[]{:S(2)}) collective-permute-start(s32[4,1000]{1,0:T(4,128)S(1)} %get-tuple-element.543), channel_id=1, source_target_pairs={{0,16},{16,0},{1,17},{17,1},{2,18},{18,2},{3,19},{19,3},{4,20},{20... | collective-permute-start | bytes 48008 | tf_op jit(solution)/shard_map/ppermute | solution.py:17
  55.4 6.2 %copy-start.27 = (s32[2,3,512]{2,1,0:T(4,128)}, s32[2,3,512]{2,1,0:T(4,128)S(1)}, u32[]{:S(2)}) copy-start(s32[2,3,512]{2,1,0:T(4,128)S(1)} %get-tuple-element.815) | copy-start | bytes 36868 | tf_op jit(solution)/shard_map/while
  55.4 6.2 %copy-start.31 = (s32[2]{0:T(128)}, s32[2]{0:T(128)S(1)}, u32[]{:S(2)}) copy-start(s32[2]{0:T(128)S(1)} %get-tuple-element.814) | copy-start | bytes 28 | tf_op jit(solution)/shard_map/while
  55.4 6.2 %copy-start.36 = (s32[2]{0:T(128)}, s32[2]{0:T(128)S(1)}, u32[]{:S(2)}) copy-start(s32[2]{0:T(128)S(1)} %get-tuple-element.817) | copy-start | bytes 28 | tf_op jit(solution)/shard_map/while
  55.4 6.2 %copy-start.38 = (s32[2]{0:T(128)}, s32[2]{0:T(128)S(1)}, u32[]{:S(2)}) copy-start(s32[2]{0:T(128)S(1)} %get-tuple-element.816) | copy-start | bytes 28 | tf_op jit(solution)/shard_map/while
  55.4 6.2 %copy-start.40 = (s32[2]{0:T(128)}, s32[2]{0:T(128)S(1)}, u32[]{:S(2)}) copy-start(s32[2]{0:T(128)S(1)} %get-tuple-element.820) | copy-start | bytes 28 | tf_op jit(solution)/shard_map/while
  55.4 8.9 %copy-start.25 = (s32[2,4,1000]{2,1,0:T(4,128)}, s32[2,4,1000]{2,1,0:T(4,128)S(1)}, u32[]{:S(2)}) copy-start(s32[2,4,1000]{2,1,0:T(4,128)S(1)} %get-tuple-element.821) | copy-start | bytes 96004 | tf_op jit(solution)/shard_map/while
  61.8 5.2 copy-start.5
  73.5 3.5 copy-start.6
  73.5 3.5 copy-start.10
  73.5 3.5 copy-start.14
  80.6 4.0 copy-start.3
  88.7 6.9 %copy-start.26 = (s32[2,4,1000]{2,1,0:T(4,128)S(1)}, s32[2,4,1000]{2,1,0:T(4,128)}, u32[]{:S(2)}) copy-start(s32[2,4,1000]{2,1,0:T(4,128)} %copy-done.25) | copy-start | bytes 96004 | tf_op jit(solution)/shard_map/while
  88.7 6.9 %copy-start.28 = (s32[2,3,512]{2,1,0:T(4,128)S(1)}, s32[2,3,512]{2,1,0:T(4,128)}, u32[]{:S(2)}) copy-start(s32[2,3,512]{2,1,0:T(4,128)} %copy-done.27) | copy-start | bytes 36868 | tf_op jit(solution)/shard_map/while
  88.8 6.9 %copy-start.32 = (s32[2]{0:T(128)S(1)}, s32[2]{0:T(128)}, u32[]{:S(2)}) copy-start(s32[2]{0:T(128)} %copy-done.31) | copy-start | bytes 28 | tf_op jit(solution)/shard_map/while
  88.8 6.9 %copy-start.37 = (s32[2]{0:T(128)S(1)}, s32[2]{0:T(128)}, u32[]{:S(2)}) copy-start(s32[2]{0:T(128)} %copy-done.36) | copy-start | bytes 28 | tf_op jit(solution)/shard_map/while
  88.8 6.9 %copy-start.39 = (s32[2]{0:T(128)S(1)}, s32[2]{0:T(128)}, u32[]{:S(2)}) copy-start(s32[2]{0:T(128)} %copy-done.38) | copy-start | bytes 28 | tf_op jit(solution)/shard_map/while
  88.8 6.9 %copy-start.41 = (s32[2]{0:T(128)S(1)}, s32[2]{0:T(128)}, u32[]{:S(2)}) copy-start(s32[2]{0:T(128)} %copy-done.40) | copy-start | bytes 28 | tf_op jit(solution)/shard_map/while
  95.7 6.2 %copy-start.27 = (s32[2,3,512]{2,1,0:T(4,128)}, s32[2,3,512]{2,1,0:T(4,128)S(1)}, u32[]{:S(2)}) copy-start(s32[2,3,512]{2,1,0:T(4,128)S(1)} %get-tuple-element.815) | copy-start | bytes 36868 | tf_op jit(solution)/shard_map/while
  95.7 6.2 %copy-start.31 = (s32[2]{0:T(128)}, s32[2]{0:T(128)S(1)}, u32[]{:S(2)}) copy-start(s32[2]{0:T(128)S(1)} %get-tuple-element.814) | copy-start | bytes 28 | tf_op jit(solution)/shard_map/while
  95.7 6.2 %copy-start.36 = (s32[2]{0:T(128)}, s32[2]{0:T(128)S(1)}, u32[]{:S(2)}) copy-start(s32[2]{0:T(128)S(1)} %get-tuple-element.817) | copy-start | bytes 28 | tf_op jit(solution)/shard_map/while
  95.7 6.2 %copy-start.38 = (s32[2]{0:T(128)}, s32[2]{0:T(128)S(1)}, u32[]{:S(2)}) copy-start(s32[2]{0:T(128)S(1)} %get-tuple-element.816) | copy-start | bytes 28 | tf_op jit(solution)/shard_map/while
  95.7 6.2 %copy-start.40 = (s32[2]{0:T(128)}, s32[2]{0:T(128)S(1)}, u32[]{:S(2)}) copy-start(s32[2]{0:T(128)S(1)} %get-tuple-element.820) | copy-start | bytes 28 | tf_op jit(solution)/shard_map/while
  95.7 8.9 %copy-start.25 = (s32[2,4,1000]{2,1,0:T(4,128)}, s32[2,4,1000]{2,1,0:T(4,128)S(1)}, u32[]{:S(2)}) copy-start(s32[2,4,1000]{2,1,0:T(4,128)S(1)} %get-tuple-element.821) | copy-start | bytes 96004 | tf_op jit(solution)/shard_map/while
  102.2 5.2 copy-start.5
  113.8 3.5 copy-start.6
  113.8 3.5 copy-start.10
  113.8 3.5 copy-start.14
  121.0 4.0 copy-start.3
  129.1 6.9 %copy-start.26 = (s32[2,4,1000]{2,1,0:T(4,128)S(1)}, s32[2,4,1000]{2,1,0:T(4,128)}, u32[]{:S(2)}) copy-start(s32[2,4,1000]{2,1,0:T(4,128)} %copy-done.25) | copy-start | bytes 96004 | tf_op jit(solution)/shard_map/while
  129.1 6.9 %copy-start.28 = (s32[2,3,512]{2,1,0:T(4,128)S(1)}, s32[2,3,512]{2,1,0:T(4,128)}, u32[]{:S(2)}) copy-start(s32[2,3,512]{2,1,0:T(4,128)} %copy-done.27) | copy-start | bytes 36868 | tf_op jit(solution)/shard_map/while
  129.1 6.9 %copy-start.32 = (s32[2]{0:T(128)S(1)}, s32[2]{0:T(128)}, u32[]{:S(2)}) copy-start(s32[2]{0:T(128)} %copy-done.31) | copy-start | bytes 28 | tf_op jit(solution)/shard_map/while
  129.1 6.9 %copy-start.37 = (s32[2]{0:T(128)S(1)}, s32[2]{0:T(128)}, u32[]{:S(2)}) copy-start(s32[2]{0:T(128)} %copy-done.36) | copy-start | bytes 28 | tf_op jit(solution)/shard_map/while
  129.1 6.9 %copy-start.39 = (s32[2]{0:T(128)S(1)}, s32[2]{0:T(128)}, u32[]{:S(2)}) copy-start(s32[2]{0:T(128)} %copy-done.38) | copy-start | bytes 28 | tf_op jit(solution)/shard_map/while
  129.1 6.9 %copy-start.41 = (s32[2]{0:T(128)S(1)}, s32[2]{0:T(128)}, u32[]{:S(2)}) copy-start(s32[2]{0:T(128)} %copy-done.40) | copy-start | bytes 28 | tf_op jit(solution)/shard_map/while
  137.8 2.2 copy-start.33
  137.8 2.8 copy-start.35
  137.8 9.4 %copy-start.2 = (f32[1345,200]{1,0:T(8,128)S(1)}, f32[1345,200]{1,0:T(8,128)}, u32[]{:S(2)}) copy-start(f32[1345,200]{1,0:T(8,128)} %get-tuple-element.377) | copy-start | bytes 3228004
  140.0 28.7 %collective-permute-start.4 = (f32[1024,200]{0,1:T(8,128)}, f32[1024,200]{0,1:T(8,128)}, u32[]{:S(2)}, u32[]{:S(2)}) collective-permute-start(f32[1024,200]{0,1:T(8,128)} %slice.233), channel_id=1, source_target_pairs={{0,16},{16,0},{1,17},{17,1},{2,18},{18,2},{3,19},{19,3},{4,20},{20... | collective-permute-start | bytes 2457608 | tf_op jit(solution)/shard_map/ppermute | solution.py:17
  140.0 1.4 collective-permute-start.5
  140.0 5.9 collective-permute-start.6
  140.5 6.1 collective-permute-start.8
  147.2 21.5 %copy-start.17 = (f32[2048,200]{0,1:T(8,128)S(1)}, f32[2048,200]{0,1:T(8,128)}, u32[]{:S(2)}) copy-start(f32[2048,200]{0,1:T(8,128)} %copy.92) | copy-start | bytes 4915204
  148.6 21.4 %copy-start.34 = (f32[1024]{0:T(1024)S(1)}, f32[1024]{0:T(1024)}, u32[]{:S(2)}) copy-start(f32[1024]{0:T(1024)} %param.12) | copy-start | bytes 12292
  148.6 21.4 %copy-start.24 = (f32[1024,200]{0,1:T(8,128)S(1)}, f32[1024,200]{0,1:T(8,128)}, u32[]{:S(2)}) copy-start(f32[1024,200]{0,1:T(8,128)} %param.11) | copy-start | bytes 2457604
  148.6 446.1 %all-reduce.5.cloned.1.call-start = ((), (), s32[]{:S(2)}) async-start(), calls=%async_computation.1 | async-start | bytes 2252800 | tf_op jit(solution)/shard_map/psum | solution.py:172
  170.0 149.4 %copy-start.29 = (f32[1345]{0:T(1024)S(1)}, f32[1345]{0:T(1024)}, u32[]{:S(2)}) copy-start(f32[1345]{0:T(1024)} %param.14) | copy-start | bytes 16144
  172.3 147.1 %copy-start.21 = (f32[1345,200]{0,1:T(8,128)S(1)}, f32[1345,200]{0,1:T(8,128)}, u32[]{:S(2)}) copy-start(f32[1345,200]{0,1:T(8,128)} %param.13) | copy-start | bytes 3228004
  172.3 150.1 %collective-permute-start.7 = (f32[1024,200]{0,1:T(8,128)}, f32[1024,200]{0,1:T(8,128)}, u32[]{:S(2)}, u32[]{:S(2)}) collective-permute-start(f32[1024,200]{0,1:T(8,128)} %divide_subtract_fusion.3), channel_id=1, source_target_pairs={{0,1},{1,0},{2,3},{3,2},{4,5},{5,4},{6,7},{7,6},{8,9},{9,8},{10,11... | collective-permute-start | bytes 2457608 | tf_op jit(solution)/shard_map/ppermute | solution.py:17
  320.9 3.1 copy-start.19
  338.2 5.2 copy-start.7
  349.8 3.5 copy-start.8
  349.8 3.5 copy-start.12
  349.9 3.5 copy-start.16
  357.0 4.0 copy-start.4
  376.5 219.7 %copy-start.30 = (f32[1345]{0:T(1024)S(1)}, f32[1345]{0:T(1024)}, u32[]{:S(2)}) copy-start(f32[1345]{0:T(1024)} %param.14) | copy-start | bytes 16144
  376.5 220.3 %copy-start.20 = (f32[1345,200]{0,1:T(8,128)S(1)}, f32[1345,200]{0,1:T(8,128)}, u32[]{:S(2)}) copy-start(f32[1345,200]{0,1:T(8,128)} %copy-done.19) | copy-start | bytes 3228004
  377.8 220.2 %collective-permute-start.9 = (f32[1024,200]{0,1:T(8,128)S(1)}, f32[1024,200]{0,1:T(8,128)S(1)}, u32[]{:S(2)}, u32[]{:S(2)}) collective-permute-start(f32[1024,200]{0,1:T(8,128)S(1)} %slice.235), channel_id=1, source_target_pairs={{0,1},{1,0},{2,3},{3,2},{4,5},{5,4},{6,7},{7,6},{8,9},{9,8},{10,11... | collective-permute-start | bytes 2457608 | tf_op jit(solution)/shard_map/ppermute | solution.py:17
  594.7 2.1 copy-start.22
  (10 other events, 14.9 us)
Sparse Core Ops, SparseCore 0:
  148.8 169.2 all-reduce.2
  374.8 219.8 all-reduce.4
where the time goes:
time: 611 us; the launch traced here: 609 us
  waiting for transfers between devices  411 us (67%)
  local copies, waits for them, and re-layouts  79.5 us (13%)
  other arithmetic  74.5 us (12%)
  between operations  16.9 us (3%)
  matrix products  16.4 us (3%)
  starting transfers between devices  7.76 us (1%)
    psum x2, waiting for transfers between devices, body(): relation_total = lax.psum(relation_grads, 'dom')  363 us
    ppermute x10, waiting for transfers between devices, swapped(): return lax.ppermute(block, axis, route)  47.9 us
    scatter-add x9, other arithmetic, block_terms(): grad_table = grad_table.at[source].add(source_grad).at[target].add(target...  32.7 us
    while x8, local copies, waits for them, and re-layouts, bucket_pass(): return lax.fori_loop(first, last, visit, carry)  15.6 us
    gather x3, local copies, waits for them, and re-layouts, block_terms(): neg_rows = table[negative_ids]  15.5 us
  transfers between devices with their start and end apart: 12, of which 6 were waited for; matrix products, arithmetic and copies ran while one was open for 5% of the time, Pallas kernels for 0%

commit v1 on v0

--- a/solution.py
+++ b/solution.py
@@ -169,7 +169,12 @@
             last,
         )
         returned = swapped(grads[rows:], "dom", bit)
-        relation_total = lax.psum(relation_grads, "dom")
+
+        def extend_the_point(inputs):
+            a_next = jnp.sum(jax.lax.all_gather(inputs, "dom"), axis=0)
+            return a_next
+
+        relation_total = extend_the_point(relation_grads)
         entities, entity_state = adagrad(entities, entity_state, grads[:rows] + returned)
         relations, relation_state = adagrad(relations, relation_state, relation_total)
     return (entities, entity_state, relations, relation_state)

time: 611 us -> 841 us (1.38)
  waiting for transfers between devices: 411 us -> 577 us
  other arithmetic: 74.5 us -> 108 us
  local copies, waits for them, and re-layouts: 79.5 us -> 110 us
    all_gather x0 -> x2, waiting for transfers between devices: none -> 515 us  [extend_the_point(): a_next = jnp.sum(jax.lax.all_gather(inputs, 'dom'), axis=0)]
    psum x2 -> x0, waiting for transfers between devices: 363 us -> none  [body(): relation_total = lax.psum(relation_grads, 'dom')]
    reduce_sum x0 -> x2, other arithmetic: none -> 27 us  [extend_the_point(): a_next = jnp.sum(jax.lax.all_gather(inputs, 'dom'), axis=0)]
    ppermute x10, waiting for transfers between devices: 47.9 us -> 62.4 us  [swapped(): return lax.ppermute(block, axis, route)]
    while x108 -> x58, local copies, waits for them, and re-layouts: 1.42 us -> 12.8 us
  transfers between devices with their start and end apart: 12 -> 12, of which waited for: 6 -> 6; matrix products, arithmetic and copies ran while one was open for 5% -> 3% of each run, Pallas kernels for 0% -> 0%
where the time goes in v1:
time: 841 us; the launch traced here: 837 us
  waiting for transfers between devices  577 us (69%)
  local copies, waits for them, and re-layouts  110 us (13%)
  other arithmetic  108 us (13%)
  between operations  16.9 us (2%)
  matrix products  14.3 us (2%)
  starting transfers between devices  8.75 us (1%)
    all_gather x2, waiting for transfers between devices, extend_the_point(): a_next = jnp.sum(jax.lax.all_gather(inputs, 'dom'), axis=0)  515 us
    ppermute x10, waiting for transfers between devices, swapped(): return lax.ppermute(block, axis, route)  62.4 us
    scatter-add x9, other arithmetic, block_terms(): grad_table = grad_table.at[source].add(source_grad).at[target].add(target...  32.8 us
    reduce_sum x2, other arithmetic, extend_the_point(): a_next = jnp.sum(jax.lax.all_gather(inputs, 'dom'), axis=0)  27 us
  transfers between devices with their start and end apart: 12, of which 6 were waited for; matrix products, arithmetic and copies ran while one was open for 3% of the time, Pallas kernels for 0%

profile of v1, /device:TPU:0, one launch (start us, length us, event | category | flops | bytes accessed | tf_op | source)
XLA Modules:
  0.0 836.8 jit_solution(1819038853900316490)
XLA Ops:
  8.6 4.1 collective-permute-start.3
  14.0 2.9 collective-permute-start
  18.3 1.7 copy.87
  20.6 30.8 %collective-permute-done = s32[1]{0:T(128)} collective-permute-done((s32[1]{0:T(128)}, s32[1]{0:T(128)}, u32[]{:S(2)}, u32[]{:S(2)}) %collective-permute-start) | collective-permute-done | bytes 36 | tf_op jit(solution)/shard_map/ppermute | solution.py:17
  51.4 1.9 and_select_fusion.1
  57.9 1.8 copy.86
  61.0 106.5 %while.30 = (s32[]{:T(128)}, f32[2048,200]{1,0:T(8,128)S(1)}, f32[1345,200]{1,0:T(8,128)}, s32[]{:T(128)}, s32[2]{0:T(128)S(1)}, /*index=5*/s32[2,3,512]{2,1,0:T...) while((s32[]{:T(128)}, f32[2048,200]{1,0:T(8,128)S(1)}, ...), condition=%wide.region_6.7_spmd, body=%wide.region_0.6_spmd.sunk | while | flops 922911104 | bytes 24889796 | solution.py:110
  65.7 3.0 gather_fusion
  68.7 1.7 fusion.63
  71.3 1.6 copy.137
  74.3 1.7 fusion.64
  79.4 2.3 gather_fusion.2
  85.2 5.2 gather_fusion.1
  91.4 1.8 convolution_add_fusion.4
  94.0 2.0 scatter_fusion
  96.2 2.0 scatter_fusion.1
  98.2 2.0 fusion.66
  100.3 6.8 scatter_fusion.2
  107.1 1.6 pad_maximum_fusion.23
  108.7 1.6 copy.143
  110.3 4.0 scatter_fusion.3
  119.0 3.0 gather_fusion
  121.9 1.7 fusion.63
  124.6 1.6 copy.137
  127.5 1.7 fusion.64
  132.6 2.3 gather_fusion.2
  138.4 5.2 gather_fusion.1
  144.6 1.8 convolution_add_fusion.4
  147.3 2.0 scatter_fusion
  149.4 2.0 scatter_fusion.1
  151.5 2.0 fusion.66
  153.5 6.8 scatter_fusion.2
  160.4 1.6 pad_maximum_fusion.23
  161.9 1.6 copy.143
  163.6 4.0 scatter_fusion.3
  167.6 2.8 copy.91
  170.6 1.7 copy.88
  173.8 28.7 %collective-permute-done.4 = f32[1024,200]{0,1:T(8,128)S(1)} collective-permute-done((f32[1024,200]{0,1:T(8,128)S(1)}, f32[1024,200]{0,1:T(8,128)S(1)}, u32[]{:S(2)}, u32[]{:S(2)}) %collective-permute-start.4) | collective-permute-done | bytes 819232 | tf_op jit(solution)/shard_map/ppermute | solution.py:17
  205.5 1.9 and_select_fusion
  212.5 2.8 copy.94
  215.4 216.1 %all-gather.7.cloned.1.call-done = f32[32,1345,200]{1,2,0:T(8,128)} async-done(((f32[1,1345,200]{1,2,0:T(8,128)}), f32[32,1345,200]{1,2,0:T(8,128)}) %all-gather.7.cloned.1.call-update) | async-done | bytes 34432016 | tf_op jit(solution)/shard_map/all_gather | solution.py:174
  431.5 13.5 %reduce_sum.81 = f32[1345,200]{0,1:T(8,128)} reduce(f32[32,1345,200]{1,2,0:T(8,128)} %all-gather.7.cloned.1.call-done, f32[]{:T(128)} %constant.415.clone.1), dimensions={0}, to_apply=%region_8.9 | reduce | flops 8339000 | bytes 35508004 | tf_op jit(solution)/shard_map/reduce_sum | solution.py:174
  445.0 1.7 copy.110
  450.1 50.8 %while.31 = (s32[]{:T(128)}, f32[2048,200]{1,0:T(8,128)S(1)}, f32[1345,200]{1,0:T(8,128)}, s32[]{:T(128)}, s32[2]{0:T(128)}, /*index=5*/s32[2,3,512]{2,1,0:T(4,1...) while((s32[]{:T(128)}, f32[2048,200]{1,0:T(8,128)S(1)}, ...), condition=%wide.region_16.17_spmd, body=%wide.region_10.16_spmd.sunk | while | flops 922911104 | bytes 20381008 | solution.py:110
  456.0 3.0 gather_fusion.4
  459.0 1.7 fusion.72
  461.6 1.6 copy.145
  466.7 2.3 gather_fusion.6
  471.8 5.2 gather_fusion.5
  478.0 1.8 convolution_add_fusion.5
  480.7 2.0 scatter_fusion.4
  482.8 2.0 scatter_fusion.5
  484.9 2.0 fusion.75
  486.9 6.8 scatter_fusion.6
  493.8 1.6 pad_maximum_fusion.27
  495.3 1.6 copy.151
  497.0 4.0 scatter_fusion.7
  500.9 2.8 copy.97
  503.7 1.7 copy.95
  507.2 2.1 collective-permute-done.9
  511.1 298.6 %all-gather.9.cloned.1.call-done = f32[32,1345,200]{1,2,0:T(8,128)} async-done(((f32[1,1345,200]{1,2,0:T(8,128)}), f32[32,1345,200]{1,2,0:T(8,128)}) %all-gather.9.cloned.1.call-update) | async-done | bytes 34432016 | tf_op jit(solution)/shard_map/all_gather | solution.py:174
  809.8 13.5 %reduce_sum.84 = f32[1345,200]{0,1:T(8,128)} reduce(f32[32,1345,200]{1,2,0:T(8,128)} %all-gather.9.cloned.1.call-done, f32[]{:T(128)} %constant.415.clone.1), dimensions={0}, to_apply=%region_18.19 | reduce | flops 8339000 | bytes 35508004 | tf_op jit(solution)/shard_map/reduce_sum | solution.py:174
  823.3 1.7 copy.111
  827.2 2.8 copy.99
  (201 shorter events, 71.8 us)
Async XLA Ops:
  7.2 424.3 %all-gather.7.cloned.1.call-start = ((), (), s32[]{:S(2)}) async-start(), calls=%async_computation | async-start | bytes 37171200 | tf_op jit(solution)/shard_map/all_gather | solution.py:174
  8.6 47.2 %collective-permute-start.3 = (s32[4,1000]{1,0:T(4,128)S(1)}, s32[4,1000]{1,0:T(4,128)S(1)}, u32[]{:S(2)}, u32[]{:S(2)}) collective-permute-start(s32[4,1000]{1,0:T(4,128)S(1)} %get-tuple-element.547), channel_id=1, source_target_pairs={{0,16},{16,0},{1,17},{17,1},{2,18},{18,2},{3,19},{19,3},{4,20},{20... | collective-permute-start | bytes 48008 | tf_op jit(solution)/shard_map/ppermute | solution.py:17
  12.6 43.8 %collective-permute-start.2 = (f32[1024,200]{0,1:T(8,128)}, f32[1024,200]{0,1:T(8,128)}, u32[]{:S(2)}, u32[]{:S(2)}) collective-permute-start(f32[1024,200]{0,1:T(8,128)} %param.11), channel_id=1, source_target_pairs={{0,16},{16,0},{1,17},{17,1},{2,18},{18,2},{3,19},{19,3},{4,20},{20... | collective-permute-start | bytes 2457608 | tf_op jit(solution)/shard_map/ppermute | solution.py:17
  14.0 37.4 %collective-permute-start = (s32[1]{0:T(128)}, s32[1]{0:T(128)}, u32[]{:S(2)}, u32[]{:S(2)}) collective-permute-start(s32[1]{0:T(128)} %bitcast.24), channel_id=1, source_target_pairs={{0,16},{16,0},{1,17},{17,1},{2,18},{18,2},{3,19},{19,3},{4,20},{20... | collective-permute-start | bytes 20 | tf_op jit(solution)/shard_map/ppermute | solution.py:17
  18.2 36.9 %collective-permute-start.1 = (s32[3,512]{1,0:T(4,128)S(1)}, s32[3,512]{1,0:T(4,128)S(1)}, u32[]{:S(2)}, u32[]{:S(2)}) collective-permute-start(s32[3,512]{1,0:T(4,128)S(1)} %bitcast.130), channel_id=1, source_target_pairs={{0,16},{16,0},{1,17},{17,1},{2,18},{18,2},{3,19},{19,3},{4,20},{20... | collective-permute-start | bytes 18440 | tf_op jit(solution)/shard_map/ppermute | solution.py:17
  61.0 16.5 %copy-start.2 = (f32[1345,200]{1,0:T(8,128)}, f32[1345,200]{1,0:T(8,128)S(1)}, u32[]{:S(2)}) copy-start(f32[1345,200]{1,0:T(8,128)S(1)} %get-tuple-element.823) | copy-start | bytes 3228004 | tf_op jit(solution)/shard_map/while
  78.5 6.7 copy-start.9
  90.4 2.8 copy-start.6
  90.4 2.8 copy-start.8
  90.4 2.8 copy-start.10
  91.4 1.8 copy-start
  100.3 6.9 copy-start.17
  107.1 7.2 copy-start.3
  114.3 16.5 %copy-start.2 = (f32[1345,200]{1,0:T(8,128)}, f32[1345,200]{1,0:T(8,128)S(1)}, u32[]{:S(2)}) copy-start(f32[1345,200]{1,0:T(8,128)S(1)} %get-tuple-element.823) | copy-start | bytes 3228004 | tf_op jit(solution)/shard_map/while
  131.7 6.7 copy-start.9
  143.6 2.8 copy-start.6
  143.6 2.8 copy-start.8
  143.6 2.8 copy-start.10
  144.6 1.8 copy-start
  153.5 6.9 copy-start.17
  160.4 7.2 copy-start.3
  170.4 639.4 %all-gather.9.cloned.1.call-start = ((), (), s32[]{:S(2)}) async-start(), calls=%async_computation.1 | async-start | bytes 37171200 | tf_op jit(solution)/shard_map/all_gather | solution.py:174
  172.3 30.2 %copy-start.14 = (f32[2048,200]{0,1:T(8,128)S(1)}, f32[2048,200]{0,1:T(8,128)}, u32[]{:S(2)}) copy-start(f32[2048,200]{0,1:T(8,128)} %copy.88) | copy-start | bytes 4915204
  172.3 30.3 %copy-start.26 = (f32[1024]{0:T(1024)S(1)}, f32[1024]{0:T(1024)}, u32[]{:S(2)}) copy-start(f32[1024]{0:T(1024)} %param.12) | copy-start | bytes 12292
  172.3 30.4 %copy-start.19 = (f32[1024,200]{0,1:T(8,128)S(1)}, f32[1024,200]{0,1:T(8,128)}, u32[]{:S(2)}) copy-start(f32[1024,200]{0,1:T(8,128)} %param.11) | copy-start | bytes 2457604
  173.7 28.8 %collective-permute-start.4 = (f32[1024,200]{0,1:T(8,128)S(1)}, f32[1024,200]{0,1:T(8,128)S(1)}, u32[]{:S(2)}, u32[]{:S(2)}) collective-permute-start(f32[1024,200]{0,1:T(8,128)S(1)} %slice.233), channel_id=1, source_target_pairs={{0,16},{16,0},{1,17},{17,1},{2,18},{18,2},{3,19},{19,3},{4,20},{20... | collective-permute-start | bytes 2457608 | tf_op jit(solution)/shard_map/ppermute | solution.py:17
  202.7 0.9 copy-start.28
  202.7 1.0 copy-start.25
  202.7 8.0 copy-start.22
  203.0 9.6 %copy-start.15 = (f32[1024,200]{0,1:T(8,128)}, f32[1024,200]{0,1:T(8,128)S(1)}, u32[]{:S(2)}) copy-start(f32[1024,200]{0,1:T(8,128)S(1)} %divide_subtract_fusion.3) | copy-start | bytes 2457604
  203.0 8.3 collective-permute-start.7
  203.1 2.5 collective-permute-start.5
  203.6 7.1 collective-permute-start.8
  203.6 6.4 collective-permute-start.6
  445.0 2.0 copy-start.23
  447.0 1.4 copy-start.20
  448.4 1.8 copy-start.4
  464.6 4.6 copy-start.29
  465.8 6.0 copy-start.11
  477.0 2.8 copy-start.7
  477.0 2.8 copy-start.12
  478.0 1.8 copy-start.1
  486.9 6.9 copy-start.18
  493.8 7.2 copy-start.5
  505.5 3.8 copy-start.13
  505.5 3.9 copy-start.27
  505.5 4.5 copy-start.16
  506.8 2.4 collective-permute-start.9
  823.3 2.0 copy-start.21
  823.3 2.0 copy-start.24
Sparse Core Ops, SparseCore 0:
  170.5 260.9 all-gather.6
  503.8 305.8 all-gather.8
